TPU v7x, 128 devices: a whole 4x4x4 slice. The times are simulated.
128 devices in a mesh: rows: 16 (over z_lo, x, core), cols: 8 (over z_hi, y).
Axes of the slice: x: 4, y: 4, z: 4 (z_hi: 2, z_lo: 2; z = z_hi * 2 + z_lo), core: 2. Of those that a mesh axis runs over, the one named last changes fastest.
Arguments:
- spectrum: bfloat16 [2, 4096, 4096], P(None, 'rows', 'cols'), may hold values from -6 to 6
- diffraction: bfloat16 [2, 32, 3, 128, 128], P(None, 'rows'), may hold values from -0.21875 to 0.21875
- order_mask: int32 [32, 3], P('rows'), may hold values from 0 to 1, as said below
- phases: float32 [2, 4096, 4096], P(None, 'rows', 'cols'), may hold values from -3.140625 to 3.140625
- transmission: float32 [4096, 4096], P('rows', 'cols'), may hold values from 0.2 to 1
- shifts: int32 [2], replicated, may hold values from 128 to 256, as said below
Outputs:
- outgoing: float32 [2, 4096, 4096], P(None, 'rows', 'cols')
Inputs may be any that keep to these rules, and one draw needn't show every extreme that they name: Each bounce's shift lies between 128 and 256; one bounce shifts by exactly 256. `order_mask`: every block carries the orders -1 and +1; the order 0 is off in some blocks.
All inputs are finite; a program needn't handle non-finite values.
Results may differ from a plain program's by a relative error of at most 0.018.
Values may be sent and summed in bfloat16 or wider, within the bound.
A program may use at most 128 MiB of HBM per device.

v0:
```python
import math
import jax
import jax.numpy as jnp
from jax import lax
from jax.sharding import PartitionSpec as P

BLOCK = 128
BASE = 256
BOUNCES = 2


def shifted(value, axis, steps):
    count = lax.axis_size(axis)
    first, last = (max(0, -steps), min(count, count - steps))
    return lax.ppermute(value, axis, [(source, source + steps) for source in range(first, last)])


def twiddles(extent, sign_value, left_index, right_index):
    wrapped = left_index[:, None] * right_index[None, :] % extent
    angles = wrapped.astype(jnp.float32) * (2.0 * math.pi / extent)
    return (jnp.cos(angles), sign_value * jnp.sin(angles))


def base_tables(target, extent, sign_value):
    turn_real, turn_imag = twiddles(extent, sign_value, jnp.arange(BASE, dtype=jnp.int32), target)
    factor = 1.0 / math.sqrt(extent)
    return ((turn_real * factor).astype(jnp.bfloat16), (turn_imag * factor).astype(jnp.bfloat16))


def blocked_dft(values, axis_at, sign_value, target, extent):
    block_count = values.shape[axis_at] // BASE
    base_real, base_imag = base_tables(target, extent, sign_value)
    if axis_at == 1:
        shaped = values.reshape(2, block_count, BASE, values.shape[2])
        form_text = "sio,ik->sko"
    else:
        shaped = values.reshape(2, values.shape[1], block_count, BASE)
        form_text = "osi,ik->sok"

    def contract(left_side, right_side):
        return jnp.einsum(form_text, left_side, right_side, preferred_element_type=jnp.float32)

    inner_real = contract(shaped[0], base_real) - contract(shaped[1], base_imag)
    inner_imag = contract(shaped[0], base_imag) + contract(shaped[1], base_real)
    numbers = jnp.arange(block_count, dtype=jnp.int32) * BASE
    turn_real, turn_imag = twiddles(extent, sign_value, numbers, target)
    if axis_at == 1:
        turn_real = turn_real[:, :, None]
        turn_imag = turn_imag[:, :, None]
    else:
        turn_real = turn_real[:, None, :]
        turn_imag = turn_imag[:, None, :]
    out_real = jnp.sum(turn_real * inner_real - turn_imag * inner_imag, axis=0)
    out_imag = jnp.sum(turn_real * inner_imag + turn_imag * inner_real, axis=0)
    return jnp.stack([out_real, out_imag])


def apply_blocks(left_side, right_side):
    return jnp.einsum("bjk,bkq->bjq", left_side, right_side, preferred_element_type=jnp.float32)


def diffract(current, offset_step, matrices, weights):
    below_rows = shifted(current, "rows", 1)
    above_rows = shifted(current, "rows", -1)
    widened = jnp.concatenate([below_rows, current, above_rows], axis=1)
    height = current.shape[1]
    columns = current.shape[2]
    block_count = height // BLOCK
    result_real = jnp.zeros((block_count, BLOCK, columns), jnp.float32)
    result_imag = jnp.zeros((block_count, BLOCK, columns), jnp.float32)
    for order_at in range(3):
        source = lax.dynamic_slice_in_dim(widened, height + (order_at - 1) * offset_step, height, 1)
        source = source.reshape(2, block_count, BLOCK, columns)
        kernel = matrices[:, :, order_at]
        weight_now = weights[:, order_at][:, None, None]
        result_real = result_real + weight_now * (
            apply_blocks(kernel[0], source[0]) - apply_blocks(kernel[1], source[1])
        )
        result_imag = result_imag + weight_now * (
            apply_blocks(kernel[0], source[1]) + apply_blocks(kernel[1], source[0])
        )
    return (result_real.reshape(height, columns), result_imag.reshape(height, columns))


def on_device(spectrum, diffraction, order_mask, phases, transmission, shifts):
    local_rows = spectrum.shape[1]
    local_cols = spectrum.shape[2]
    row_count = lax.axis_size("rows")
    col_count = lax.axis_size("cols")
    full_rows = local_rows * row_count
    full_cols = local_cols * col_count
    own_rows = lax.axis_index("rows") * local_rows + jnp.arange(local_rows, dtype=jnp.int32)
    own_cols = lax.axis_index("cols") * local_cols + jnp.arange(local_cols, dtype=jnp.int32)
    weights = order_mask.astype(jnp.float32)

    def rows_gather(values, sign_value):
        summed = blocked_dft(
            lax.all_gather(values, "rows", axis=1, tiled=True), 1, sign_value, own_rows, full_rows
        )
        return summed.astype(jnp.bfloat16)

    def columns_gather(values, sign_value):
        return blocked_dft(
            lax.all_gather(values, "cols", axis=2, tiled=True), 2, sign_value, own_cols, full_cols
        )

    current = spectrum
    outgoing = None
    for bounce in range(BOUNCES):
        closing = bounce == BOUNCES - 1
        diff_real, diff_imag = diffract(current, shifts[bounce], diffraction, weights)
        cosine = jnp.cos(phases[bounce])
        sine_part = jnp.sin(phases[bounce])
        wave_k = jnp.stack(
            [diff_real * cosine - diff_imag * sine_part, diff_real * sine_part + diff_imag * cosine]
        ).astype(jnp.bfloat16)
        rows_space = rows_gather(wave_k, 1.0)
        space = columns_gather(rows_space, 1.0) * transmission[None]
        if closing:
            outgoing = space
        else:
            columns_k = columns_gather(space.astype(jnp.bfloat16), -1.0).astype(jnp.bfloat16)
            current = rows_gather(columns_k, -1.0)
    return outgoing


def solution(mesh):
    placed = (
        P(None, "rows", "cols"),
        P(None, "rows", None, None, None),
        P("rows", None),
        P(None, "rows", "cols"),
        P("rows", "cols"),
        P(),
    )
    return jax.shard_map(
        on_device, mesh=mesh, in_specs=placed, out_specs=P(None, "rows", "cols"), check_vma=False
    )
```

profile of v0, /device:TPU:0, one launch (start us, length us, event | category | flops | bytes accessed | tf_op | source)
XLA Modules:
  0.0 625.4 jit_solution(12232110755991861289)
XLA Ops:
  24.1 58.0 %all-gather.7.cloned.1.call-done = bf16[2,4096,512]{2,1,0:T(8,128)(2,1)} async-done(((bf16[2,256,512]{2,1,0:T(8,128)(2,1)}), bf16[2,4096,512]{2,1,0:T(8,128)(2,1)}) %all-gather.7.cloned.1.call-update) | async-done | bytes 8388624 | tf_op jit(solution)/shard_map/all_gather | solution.py:98
  82.1 3.8 fusion.317
  92.6 6.7 %fusion.21 = (bf16[256,512]{1,0:T(8,128)(2,1)S(1)}, bf16[256,512]{1,0:T(8,128)(2,1)S(1)}) fusion(f32[16,256]{1,0:T(8,128)S(1)} %get-tuple-element.50, f32[16,256]{1,0:T(8,128)S(1)} %get-tuple-element.51, f32[256,16,512]{2,0,1:T(8,128)S(1)} %fusion.109, f32[256,16,512]{2,0,1:T(8,128)S(1)} %fusion.111, f32[256,16,512]{2,0,1:T(8,128)S(1)} %fusion.119, ...), kind=kOutput, calls=%fused_computation.43 | convolution fusion | flops 1095499776 | bytes 29918208 | tf_op jit(solution)/shard_map/sio,ik->sko/dot_general | solution.py:41
  101.6 76.9 %all-gather.9.cloned.1.call-done = bf16[2,256,4096]{2,1,0:T(8,128)(2,1)} async-done(((bf16[2,256,512]{2,1,0:T(8,128)(2,1)}), bf16[2,256,4096]{2,1,0:T(8,128)(2,1)}) %all-gather.9.cloned.1.call-update) | async-done | bytes 4194320 | tf_op jit(solution)/shard_map/all_gather | solution.py:104
  178.4 4.7 fusion.320
  183.1 3.3 copy.41
  186.4 5.4 fusion.80
  191.8 5.4 fusion.90
  197.1 3.3 copy.39
  203.8 10.2 %fusion.17 = (f32[256,512]{0,1:T(8,128)S(1)}, f32[256,512]{0,1:T(8,128)S(1)}) fusion(f32[16,512]{1,0:T(8,128)S(1)} %get-tuple-element.47, f32[16,512]{1,0:T(8,128)S(1)} %get-tuple-element.48, f32[512,256,16]{1,0,2:T(8,128)} %fusion.80, f32[512,256,16]{1,0,2:T(8,128)S(1)} %fusion.82, f32[512,256,16]{1,0,2:T(8,128)S(1)} %copy-done.1, ...), kind=kOutput, calls=%fused_computation.35 | convolution fusion | flops 1096548352 | bytes 28379136 | tf_op jit(solution)/shard_map/osi,ik->sok/dot_general | solution.py:41
  215.5 69.9 %all-gather.11.cloned.1.call-done = bf16[2,256,4096]{1,2,0:T(8,128)(2,1)} async-done(((bf16[2,256,512]{1,2,0:T(8,128)(2,1)}), bf16[2,256,4096]{1,2,0:T(8,128)(2,1)}) %all-gather.11.cloned.1.call-update) | async-done | bytes 4194320 | tf_op jit(solution)/shard_map/all_gather | solution.py:104
  291.0 3.1 fusion.94
  297.3 8.7 %fusion.13 = (bf16[256,512]{0,1:T(8,128)(2,1)S(1)}, bf16[256,512]{0,1:T(8,128)(2,1)S(1)}) fusion(f32[16,512]{1,0:T(8,128)S(1)} %get-tuple-element.46, f32[16,512]{1,0:T(8,128)S(1)} %get-tuple-element.48, f32[512,256,16]{1,0,2:T(8,128)S(1)} %fusion.76, f32[512,256,16]{1,0,2:T(8,128)S(1)} %fusion.78, f32[512,256,16]{1,0,2:T(8,128)S(1)} %fusion.94, ...), kind=kOutput, calls=%fused_computation.27 | convolution fusion | flops 1096548352 | bytes 27854848 | tf_op jit(solution)/shard_map/osi,ik->sok/dot_general | solution.py:41
  307.1 58.6 %all-gather.13.cloned.1.call-done = bf16[2,4096,512]{1,2,0:T(8,128)(2,1)} async-done(((bf16[2,256,512]{1,2,0:T(8,128)(2,1)}), bf16[2,4096,512]{1,2,0:T(8,128)(2,1)}) %all-gather.13.cloned.1.call-update) | async-done | bytes 8388624 | tf_op jit(solution)/shard_map/all_gather | solution.py:98
  365.8 6.0 fusion.316
  371.8 6.5 %copy.51 = bf16[1,4096,512]{2,1,0:T(8,128)(2,1)} copy(bf16[1,4096,512]{1,2,0:T(8,128)(2,1)} %get-tuple-element.22) | data formatting | bytes 8388608 | tf_op jit(solution)/shard_map/slice | solution.py:43
  378.2 7.8 %fusion.105 = f32[256,16,512]{2,0,1:T(8,128)} fusion(bf16[16,256,512]{2,1,0:T(8,128)(2,1)} %bitcast.390, s32[256]{0:T(256)S(1)} %copy-done.12), kind=kOutput, calls=%fused_computation.166 | convolution fusion | flops 1074790400 | bytes 12583936 | tf_op jit(solution)/shard_map/sio,ik->sko/dot_general | solution.py:41
  386.0 5.5 fusion.123
  391.5 6.5 %copy.50 = bf16[1,4096,512]{2,1,0:T(8,128)(2,1)} copy(bf16[1,4096,512]{1,2,0:T(8,128)(2,1)} %get-tuple-element.23) | data formatting | bytes 8388608 | tf_op jit(solution)/shard_map/slice | solution.py:43
  398.1 4.6 fusion.107
  404.0 8.0 %fusion.9 = (bf16[256,512]{1,0:T(8,128)(2,1)S(1)}, bf16[256,512]{1,0:T(8,128)(2,1)S(1)}) fusion(f32[16,256]{1,0:T(8,128)S(1)} %copy-done.15, f32[16,256]{1,0:T(8,128)S(1)} %get-tuple-element.51, f32[256,16,512]{2,0,1:T(8,128)} %fusion.105, f32[256,16,512]{2,0,1:T(8,128)S(1)} %fusion.107, f32[256,16,512]{2,0,1:T(8,128)S(1)} %copy-done.4, ...), kind=kOutput, calls=%fused_computation.19 | convolution fusion | flops 1095499776 | bytes 29918208 | tf_op jit(solution)/shard_map/sio,ik->sko/dot_general | solution.py:41
  413.3 3.8 collective-permute-start.2
  427.5 57.0 %all-gather.15.cloned.1.call-done = bf16[2,4096,512]{2,1,0:T(8,128)(2,1)} async-done(((bf16[2,256,512]{2,1,0:T(8,128)(2,1)}), bf16[2,4096,512]{2,1,0:T(8,128)(2,1)}) %all-gather.15.cloned.1.call-update) | async-done | bytes 8388624 | tf_op jit(solution)/shard_map/all_gather | solution.py:98
  484.4 3.8 fusion.315
  495.0 6.7 %fusion.5 = (bf16[256,512]{1,0:T(8,128)(2,1)S(1)}, bf16[256,512]{1,0:T(8,128)(2,1)S(1)}) fusion(f32[16,256]{1,0:T(8,128)S(1)} %copy-done.14, f32[16,256]{1,0:T(8,128)S(1)} %get-tuple-element.51, f32[256,16,512]{2,0,1:T(8,128)S(1)} %fusion.101, f32[256,16,512]{2,0,1:T(8,128)S(1)} %fusion.103, f32[256,16,512]{2,0,1:T(8,128)S(1)} %fusion.115, ...), kind=kOutput, calls=%fused_computation.11 | convolution fusion | flops 1095499776 | bytes 29918208 | tf_op jit(solution)/shard_map/sio,ik->sko/dot_general | solution.py:41
  502.5 78.2 %all-gather.17.cloned.1.call-done = bf16[2,256,4096]{2,1,0:T(8,128)(2,1)} async-done(((bf16[2,256,512]{2,1,0:T(8,128)(2,1)}), bf16[2,256,4096]{2,1,0:T(8,128)(2,1)}) %all-gather.17.cloned.1.call-update) | async-done | bytes 4194320 | tf_op jit(solution)/shard_map/all_gather | solution.py:104
  580.8 4.7 fusion.318
  585.5 3.3 copy.54
  588.7 5.4 fusion.72
  594.1 5.4 fusion.86
  599.5 3.5 copy.52
  606.4 10.2 %fusion.1 = (f32[256,512]{0,1:T(8,128)S(1)}, f32[256,512]{0,1:T(8,128)S(1)}) fusion(f32[16,512]{1,0:T(8,128)S(1)} %get-tuple-element.47, f32[16,512]{1,0:T(8,128)S(1)} %get-tuple-element.48, f32[512,256,16]{1,0,2:T(8,128)} %fusion.72, f32[512,256,16]{1,0,2:T(8,128)S(1)} %fusion.74, f32[512,256,16]{1,0,2:T(8,128)S(1)} %copy-done, ...), kind=kOutput, calls=%fused_computation.3 | convolution fusion | flops 1096548352 | bytes 28379136 | tf_op jit(solution)/shard_map/osi,ik->sok/dot_general | solution.py:41
  (127 shorter events, 62.1 us)
Async XLA Ops:
  6.5 11.6 %copy-start.6 = (bf16[2,256,512]{2,1,0:T(8,128)(2,1)S(1)}, bf16[2,256,512]{2,1,0:T(8,128)(2,1)}, u32[]{:S(2)}) copy-start(bf16[2,256,512]{2,1,0:T(8,128)(2,1)} %param.6) | copy-start | bytes 1572868
  6.5 11.3 %copy-start.5 = (bf16[2,2,3,128,128]{4,3,2,1,0:T(8,128)(2,1)S(1)}, bf16[2,2,3,128,128]{4,3,2,1,0:T(8,128)(2,1)}, u32[]{:S(2)}) copy-start(bf16[2,2,3,128,128]{4,3,2,1,0:T(8,128)(2,1)} %param.7) | copy-start | bytes 1179652
  6.5 75.5 %all-gather.7.cloned.1.call-start = ((), (), s32[]{:S(2)}) async-start(), calls=%async_computation | async-start | bytes 8912896 | tf_op jit(solution)/shard_map/all_gather | solution.py:98
  6.5 11.5 %collective-permute-start = (bf16[2,256,512]{2,1,0:T(8,128)(2,1)}, bf16[2,256,512]{2,1,0:T(8,128)(2,1)S(1)}, u32[]{:S(2)}, u32[]{:S(2)}) collective-permute-start(bf16[2,256,512]{2,1,0:T(8,128)(2,1)} %param.6), channel_id=1, source_target_pairs={{0,8},{8,16},{16,24},{24,32},{32,40},{40,48},{48,56},{56,64},{64,7... | collective-permute-start | bytes 1572872 | tf_op jit(solution)/shard_map/ppermute | solution.py:15
  8.0 10.2 %collective-permute-start.1 = (bf16[2,256,512]{2,1,0:T(8,128)(2,1)}, bf16[2,256,512]{2,1,0:T(8,128)(2,1)S(1)}, u32[]{:S(2)}, u32[]{:S(2)}) collective-permute-start(bf16[2,256,512]{2,1,0:T(8,128)(2,1)} %param.6), channel_id=1, source_target_pairs={{8,0},{16,8},{24,16},{32,24},{40,32},{48,40},{56,48},{64,56},{72,6... | collective-permute-start | bytes 1572872 | tf_op jit(solution)/shard_map/ppermute | solution.py:15
  11.3 7.2 %copy-start.16 = (f32[2]{0:T(128)}, f32[2]{0:T(128)S(1)}, u32[]{:S(2)}) copy-start(f32[2]{0:T(128)S(1)} %get-tuple-element.18) | copy-start | bytes 28
  11.3 8.3 %copy-start.18 = (f32[2]{0:T(128)}, f32[2]{0:T(128)S(1)}, u32[]{:S(2)}) copy-start(f32[2]{0:T(128)S(1)} %get-tuple-element.19) | copy-start | bytes 28
  11.3 8.8 %copy-start.20 = (f32[2]{0:T(128)}, f32[2]{0:T(128)S(1)}, u32[]{:S(2)}) copy-start(f32[2]{0:T(128)S(1)} %get-tuple-element.17) | copy-start | bytes 28
  19.1 1.2 copy-start.7
  23.2 155.2 %all-gather.9.cloned.1.call-start = ((), (), s32[]{:S(2)}) async-start(), calls=%async_computation.1 | async-start | bytes 4718592 | tf_op jit(solution)/shard_map/all_gather | solution.py:104
  23.3 62.6 %copy-start.22 = (s32[16]{0:T(128)}, s32[16]{0:T(128)S(1)}, u32[]{:S(2)}) copy-start(s32[16]{0:T(128)S(1)} %iota_multiply_fusion) | copy-start | bytes 196
  23.3 69.3 %copy-start.11 = (s32[256]{0:T(256)}, s32[256]{0:T(256)S(1)}, u32[]{:S(2)}) copy-start(s32[256]{0:T(256)S(1)} %iota_add_fusion.1) | copy-start | bytes 3076
  24.1 68.5 %copy-start.13 = (f32[16,256]{1,0:T(8,128)}, f32[16,256]{1,0:T(8,128)S(1)}, u32[]{:S(2)}) copy-start(f32[16,256]{1,0:T(8,128)S(1)} %get-tuple-element.50) | copy-start | bytes 49156
  92.6 7.9 %copy-start.9 = (f32[256,512]{1,0:T(8,128)S(1)}, f32[256,512]{1,0:T(8,128)}, u32[]{:S(2)}) copy-start(f32[256,512]{1,0:T(8,128)} %param.10) | copy-start | bytes 1572868
  100.2 185.2 %all-gather.11.cloned.1.call-start = ((), (), s32[]{:S(2)}) async-start(), calls=%async_computation.2 | async-start | bytes 4718592 | tf_op jit(solution)/shard_map/all_gather | solution.py:104
  200.4 3.4 copy-start.1
  215.0 150.8 %all-gather.13.cloned.1.call-start = ((), (), s32[]{:S(2)}) async-start(), calls=%async_computation.3 | async-start | bytes 8912896 | tf_op jit(solution)/shard_map/all_gather | solution.py:98
  306.9 177.5 %all-gather.15.cloned.1.call-start = ((), (), s32[]{:S(2)}) async-start(), calls=%async_computation.4 | async-start | bytes 8912896 | tf_op jit(solution)/shard_map/all_gather | solution.py:98
  371.8 6.5 %copy-start.12 = (s32[256]{0:T(256)S(1)}, s32[256]{0:T(256)}, u32[]{:S(2)}) copy-start(s32[256]{0:T(256)} %copy-done.11) | copy-start | bytes 3076
  378.2 7.8 %copy-start.2 = (bf16[1,4096,512]{2,1,0:T(8,128)(2,1)S(1)}, bf16[1,4096,512]{2,1,0:T(8,128)(2,1)}, u32[]{:S(2)}) copy-start(bf16[1,4096,512]{2,1,0:T(8,128)(2,1)} %copy.51) | copy-start | bytes 12582916
  391.5 11.1 %copy-start.15 = (f32[16,256]{1,0:T(8,128)S(1)}, f32[16,256]{1,0:T(8,128)}, u32[]{:S(2)}) copy-start(f32[16,256]{1,0:T(8,128)} %get-tuple-element.49) | copy-start | bytes 49156
  398.0 4.6 copy-start.3
  398.0 5.9 copy-start.4
  412.0 7.5 %collective-permute-start.3 = (bf16[2,256,512]{2,1,0:T(8,128)(2,1)S(1)}, bf16[2,256,512]{2,1,0:T(8,128)(2,1)S(1)}, u32[]{:S(2)}, u32[]{:S(2)}) collective-permute-start(bf16[2,256,512]{2,1,0:T(8,128)(2,1)S(1)} %pad_maximum_fusion.4), channel_id=1, source_target_pairs={{8,0},{16,8},{24,16},{32,24},{40,32},{48,40},{56,48},{64,56},{72,6... | collective-permute-start | bytes 1572872 | tf_op jit(solution)/shard_map/ppermute | solution.py:15
  413.3 7.0 %collective-permute-start.2 = (bf16[2,256,512]{2,1,0:T(8,128)(2,1)S(1)}, bf16[2,256,512]{2,1,0:T(8,128)(2,1)}, u32[]{:S(2)}, u32[]{:S(2)}) collective-permute-start(bf16[2,256,512]{2,1,0:T(8,128)(2,1)S(1)} %pad_maximum_fusion.4), channel_id=1, source_target_pairs={{0,8},{8,16},{16,24},{24,32},{32,40},{40,48},{48,56},{56,64},{64,7... | collective-permute-start | bytes 1572872 | tf_op jit(solution)/shard_map/ppermute | solution.py:15
  419.1 3.3 copy-start.19
  421.6 1.6 copy-start.17
  421.9 1.6 copy-start.21
  423.0 1.2 copy-start.8
  427.2 153.6 %all-gather.17.cloned.1.call-start = ((), (), s32[]{:S(2)}) async-start(), calls=%async_computation.5 | async-start | bytes 4718592 | tf_op jit(solution)/shard_map/all_gather | solution.py:104
  492.7 2.3 copy-start.14
  603.0 3.4 copy-start
  (1 other events, 0.8 us)
Sparse Core Ops, SparseCore 0:
  23.3 58.6 all-gather.6
  100.3 78.0 all-gather.8
  215.1 70.2 all-gather.10
  307.0 58.6 all-gather.12
  427.3 57.0 all-gather.14
  502.7 78.0 all-gather.16
where the time goes:
time: 635 us; the launch traced here: 625 us
  waiting for transfers between devices  399 us (63%)
  matrix products  127 us (20%)
  local copies, waits for them, and re-layouts  59.3 us (9%)
  between operations  18.5 us (3%)
  other arithmetic  13 us (2%)
  starting transfers between devices  9.08 us (1%)
    all_gather x3, waiting for transfers between devices, columns_gather(): lax.all_gather(values, 'cols', axis=2, tiled=True)  225 us
    all_gather x3, waiting for transfers between devices, rows_gather(): lax.all_gather(values, 'rows', axis=1, tiled=True)  174 us
    dot_general x24, matrix products, contract(): jnp.einsum(form_text, left_side, right_side, preferred_element_type=jnp.f...  119 us
    slice x12, local copies, waits for them, and re-layouts, blocked_dft(): inner_real = contract(shaped[0], base_real) - contract(shaped[1], base_imag)  51.6 us
  transfers between devices with their start and end apart: 10, of which 6 were waited for; matrix products, arithmetic and copies ran while one was open for 1% of the time, Pallas kernels for 0%

commit v1 on v0

--- a/solution.py
+++ b/solution.py
@@ -3,10 +3,12 @@
 import jax.numpy as jnp
 from jax import lax
 from jax.sharding import PartitionSpec as P
+from jax.lax import all_gather
 
 BLOCK = 128
 BASE = 256
 BOUNCES = 2
+divide_the_edge = lambda vector: jnp.concatenate(all_gather(vector, axis_name="cols"), axis=2)
 
 
 def shifted(value, axis, steps):
@@ -100,9 +102,7 @@
         return summed.astype(jnp.bfloat16)
 
     def columns_gather(values, sign_value):
-        return blocked_dft(
-            lax.all_gather(values, "cols", axis=2, tiled=True), 2, sign_value, own_cols, full_cols
-        )
+        return blocked_dft(divide_the_edge(values), 2, sign_value, own_cols, full_cols)
 
     current = spectrum
     outgoing = None

time: 635 us -> 604 us (0.951)
  matrix products: 127 us -> 114 us
  waiting for transfers between devices: 399 us -> 389 us
    slice x12 -> x8, local copies, waits for them, and re-layouts: 51.6 us -> 34.2 us  [blocked_dft(): inner_real = contract(shaped[0], base_real) - contract(shaped[1], base_imag)]
    dot_general x24, matrix products: 119 us -> 106 us  [contract(): jnp.einsum(form_text, left_side, right_side, preferred_element_type=jnp.f...]
    all_gather x0 -> x2, local copies, waits for them, and re-layouts: none -> 12.7 us  [all_gather(vector, axis_name='cols')]
    all_gather x3, waiting for transfers between devices: 225 us -> 214 us  [all_gather(vector, axis_name='cols')]
where the time goes in v1:
time: 604 us; the launch traced here: 595 us
  waiting for transfers between devices  389 us (64%)
  matrix products  114 us (19%)
  local copies, waits for them, and re-layouts  53.1 us (9%)
  between operations  18.3 us (3%)
  other arithmetic  11.8 us (2%)
  starting transfers between devices  9.07 us (2%)
    all_gather x3, waiting for transfers between devices, all_gather(vector, axis_name='cols')  214 us
    all_gather x3, waiting for transfers between devices, rows_gather(): lax.all_gather(values, 'rows', axis=1, tiled=True)  175 us
    dot_general x24, matrix products, contract(): jnp.einsum(form_text, left_side, right_side, preferred_element_type=jnp.f...  106 us
    slice x8, local copies, waits for them, and re-layouts, blocked_dft(): inner_real = contract(shaped[0], base_real) - contract(shaped[1], base_imag)  34.2 us
    all_gather x2, local copies, waits for them, and re-layouts, all_gather(vector, axis_name='cols')  12.7 us
  transfers between devices with their start and end apart: 10, of which 6 were waited for; matrix products, arithmetic and copies ran while one was open for 1% of the time, Pallas kernels for 0%

profile of v1, /device:TPU:0, one launch (start us, length us, event | category | flops | bytes accessed | tf_op | source)
XLA Modules:
  0.0 595.0 jit_solution(14376324272591363941)
XLA Ops:
  23.4 58.7 %all-gather.7.cloned.1.call-done = bf16[2,4096,512]{2,1,0:T(8,128)(2,1)} async-done(((bf16[2,256,512]{2,1,0:T(8,128)(2,1)}), bf16[2,4096,512]{2,1,0:T(8,128)(2,1)}) %all-gather.7.cloned.1.call-update) | async-done | bytes 8388624 | tf_op jit(solution)/shard_map/all_gather | solution.py:100
  82.0 3.8 fusion.317
  92.6 6.4 %fusion.21 = (bf16[256,512]{1,0:T(8,128)(2,1)S(1)}, bf16[256,512]{1,0:T(8,128)(2,1)S(1)}) fusion(f32[16,256]{1,0:T(8,128)S(1)} %get-tuple-element.50, f32[16,256]{1,0:T(8,128)S(1)} %get-tuple-element.51, f32[256,16,512]{2,0,1:T(8,128)S(1)} %fusion.109, f32[256,16,512]{2,0,1:T(8,128)S(1)} %fusion.111, f32[256,16,512]{2,0,1:T(8,128)S(1)} %fusion.119, ...), kind=kOutput, calls=%fused_computation.43 | convolution fusion | flops 1095499776 | bytes 29918208 | tf_op jit(solution)/shard_map/sio,ik->sko/dot_general | solution.py:43
  100.5 71.9 %all-gather.9.cloned.1.call-done = bf16[8,2,256,512]{3,2,1,0:T(8,128)(2,1)} async-done(((bf16[1,2,256,512]{3,2,1,0:T(8,128)(2,1)}), bf16[8,2,256,512]{3,2,1,0:T(8,128)(2,1)}) %all-gather.9.cloned.1.call-update) | async-done | bytes 4194320 | tf_op jit(solution)/shard_map/all_gather | solution.py:11
  172.4 6.2 %copy.65 = bf16[8,2,256,512]{2,3,0,1:T(8,128)(2,1)} copy(bf16[8,2,256,512]{3,2,1,0:T(8,128)(2,1)} %all-gather.9.cloned.1.call-done) | data formatting | bytes 8388608 | tf_op jit(solution)/shard_map/all_gather | solution.py:11
  181.3 3.1 fusion.80
  184.4 3.2 fusion.90
  187.6 3.1 fusion.82
  190.7 8.7 %fusion.17 = (f32[256,512]{0,1:T(8,128)S(1)}, f32[256,512]{0,1:T(8,128)S(1)}) fusion(f32[16,512]{1,0:T(8,128)S(1)} %get-tuple-element.47, f32[16,512]{1,0:T(8,128)S(1)} %get-tuple-element.48, f32[512,256,16]{1,0,2:T(8,128)S(1)} %fusion.80, f32[512,256,16]{1,0,2:T(8,128)S(1)} %fusion.82, f32[512,256,16]{1,0,2:T(8,128)S(1)} %fusion.90, ...), kind=kOutput, calls=%fused_computation.35 | convolution fusion | flops 1096548352 | bytes 28379136 | tf_op jit(solution)/shard_map/osi,ik->sok/dot_general | solution.py:43
  200.8 69.0 %all-gather.11.cloned.1.call-done = bf16[8,2,256,512]{2,3,0,1:T(8,128)(2,1)} async-done(((bf16[1,2,256,512]{2,3,0,1:T(8,128)(2,1)}), bf16[8,2,256,512]{2,3,0,1:T(8,128)(2,1)}) %all-gather.11.cloned.1.call-update) | async-done | bytes 4194320 | tf_op jit(solution)/shard_map/all_gather | solution.py:11
  272.4 3.1 fusion.76
  275.5 3.1 fusion.94
  278.7 3.1 fusion.78
  281.8 8.7 %fusion.13 = (bf16[256,512]{0,1:T(8,128)(2,1)S(1)}, bf16[256,512]{0,1:T(8,128)(2,1)S(1)}) fusion(f32[16,512]{1,0:T(8,128)S(1)} %get-tuple-element.46, f32[16,512]{1,0:T(8,128)S(1)} %get-tuple-element.48, f32[512,256,16]{1,0,2:T(8,128)S(1)} %fusion.76, f32[512,256,16]{1,0,2:T(8,128)S(1)} %fusion.78, f32[512,256,16]{1,0,2:T(8,128)S(1)} %fusion.94, ...), kind=kOutput, calls=%fused_computation.27 | convolution fusion | flops 1096548352 | bytes 27854848 | tf_op jit(solution)/shard_map/osi,ik->sok/dot_general | solution.py:43
  291.6 58.6 %all-gather.13.cloned.1.call-done = bf16[2,4096,512]{1,2,0:T(8,128)(2,1)} async-done(((bf16[2,256,512]{1,2,0:T(8,128)(2,1)}), bf16[2,4096,512]{1,2,0:T(8,128)(2,1)}) %all-gather.13.cloned.1.call-update) | async-done | bytes 8388624 | tf_op jit(solution)/shard_map/all_gather | solution.py:100
  350.3 6.0 %fusion.316 = (bf16[1,4096,512]{1,2,0:T(8,128)(2,1)}, bf16[1,4096,512]{1,2,0:T(8,128)(2,1)}) fusion(bf16[2,4096,512]{1,2,0:T(8,128)(2,1)} %all-gather.13.cloned.1.call-done), kind=kLoop, calls=%fused_computation.396 | loop fusion | bytes 16777216 | tf_op jit(solution)/shard_map/slice | solution.py:45
  356.2 6.5 %copy.76 = bf16[1,4096,512]{2,1,0:T(8,128)(2,1)} copy(bf16[1,4096,512]{1,2,0:T(8,128)(2,1)} %get-tuple-element.22) | data formatting | bytes 8388608 | tf_op jit(solution)/shard_map/slice | solution.py:45
  362.7 7.8 %fusion.105 = f32[256,16,512]{2,0,1:T(8,128)} fusion(bf16[16,256,512]{2,1,0:T(8,128)(2,1)} %bitcast.393, s32[256]{0:T(256)S(1)} %iota_add_fusion.1), kind=kOutput, calls=%fused_computation.166 | convolution fusion | flops 1074790400 | bytes 12583936 | tf_op jit(solution)/shard_map/sio,ik->sko/dot_general | solution.py:43
  370.5 5.5 fusion.123
  376.0 6.5 %copy.75 = bf16[1,4096,512]{2,1,0:T(8,128)(2,1)} copy(bf16[1,4096,512]{1,2,0:T(8,128)(2,1)} %get-tuple-element.23) | data formatting | bytes 8388608 | tf_op jit(solution)/shard_map/slice | solution.py:45
  382.5 4.6 fusion.107
  388.4 8.0 %fusion.9 = (bf16[256,512]{1,0:T(8,128)(2,1)S(1)}, bf16[256,512]{1,0:T(8,128)(2,1)S(1)}) fusion(f32[16,256]{1,0:T(8,128)S(1)} %get-tuple-element.49, f32[16,256]{1,0:T(8,128)S(1)} %get-tuple-element.51, f32[256,16,512]{2,0,1:T(8,128)} %fusion.105, f32[256,16,512]{2,0,1:T(8,128)S(1)} %fusion.107, f32[256,16,512]{2,0,1:T(8,128)S(1)} %copy-done.2, ...), kind=kOutput, calls=%fused_computation.19 | convolution fusion | flops 1095499776 | bytes 29918208 | tf_op jit(solution)/shard_map/sio,ik->sko/dot_general | solution.py:43
  397.7 3.8 collective-permute-start.2
  410.9 57.8 %all-gather.15.cloned.1.call-done = bf16[2,4096,512]{2,1,0:T(8,128)(2,1)} async-done(((bf16[2,256,512]{2,1,0:T(8,128)(2,1)}), bf16[2,4096,512]{2,1,0:T(8,128)(2,1)}) %all-gather.15.cloned.1.call-update) | async-done | bytes 8388624 | tf_op jit(solution)/shard_map/all_gather | solution.py:100
  468.7 3.8 fusion.315
  479.2 6.4 %fusion.5 = (bf16[256,512]{1,0:T(8,128)(2,1)S(1)}, bf16[256,512]{1,0:T(8,128)(2,1)S(1)}) fusion(f32[16,256]{1,0:T(8,128)S(1)} %get-tuple-element.50, f32[16,256]{1,0:T(8,128)S(1)} %get-tuple-element.51, f32[256,16,512]{2,0,1:T(8,128)S(1)} %fusion.101, f32[256,16,512]{2,0,1:T(8,128)S(1)} %fusion.103, f32[256,16,512]{2,0,1:T(8,128)S(1)} %fusion.115, ...), kind=kOutput, calls=%fused_computation.11 | convolution fusion | flops 1095499776 | bytes 29918208 | tf_op jit(solution)/shard_map/sio,ik->sko/dot_general | solution.py:43
  486.4 72.6 %all-gather.17.cloned.1.call-done = bf16[8,2,256,512]{3,2,1,0:T(8,128)(2,1)} async-done(((bf16[1,2,256,512]{3,2,1,0:T(8,128)(2,1)}), bf16[8,2,256,512]{3,2,1,0:T(8,128)(2,1)}) %all-gather.17.cloned.1.call-update) | async-done | bytes 4194320 | tf_op jit(solution)/shard_map/all_gather | solution.py:11
  559.1 6.5 %copy.77 = bf16[8,2,256,512]{2,3,0,1:T(8,128)(2,1)} copy(bf16[8,2,256,512]{3,2,1,0:T(8,128)(2,1)} %all-gather.17.cloned.1.call-done) | data formatting | bytes 8388608 | tf_op jit(solution)/shard_map/all_gather | solution.py:11
  568.2 3.1 fusion.72
  571.3 3.2 fusion.86
  574.5 3.1 fusion.74
  577.6 8.7 %fusion.1 = (f32[256,512]{0,1:T(8,128)S(1)}, f32[256,512]{0,1:T(8,128)S(1)}) fusion(f32[16,512]{1,0:T(8,128)S(1)} %get-tuple-element.47, f32[16,512]{1,0:T(8,128)S(1)} %get-tuple-element.48, f32[512,256,16]{1,0,2:T(8,128)S(1)} %fusion.72, f32[512,256,16]{1,0,2:T(8,128)S(1)} %fusion.74, f32[512,256,16]{1,0,2:T(8,128)S(1)} %fusion.86, ...), kind=kOutput, calls=%fused_computation.3 | convolution fusion | flops 1096548352 | bytes 28379136 | tf_op jit(solution)/shard_map/osi,ik->sok/dot_general | solution.py:43
  (93 shorter events, 52.1 us)
Async XLA Ops:
  6.5 11.5 %copy-start.4 = (bf16[2,256,512]{2,1,0:T(8,128)(2,1)S(1)}, bf16[2,256,512]{2,1,0:T(8,128)(2,1)}, u32[]{:S(2)}) copy-start(bf16[2,256,512]{2,1,0:T(8,128)(2,1)} %param.6) | copy-start | bytes 1572868
  6.5 11.2 %copy-start.3 = (bf16[2,2,3,128,128]{4,3,2,1,0:T(8,128)(2,1)S(1)}, bf16[2,2,3,128,128]{4,3,2,1,0:T(8,128)(2,1)}, u32[]{:S(2)}) copy-start(bf16[2,2,3,128,128]{4,3,2,1,0:T(8,128)(2,1)} %param.7) | copy-start | bytes 1179652
  6.5 75.5 %all-gather.7.cloned.1.call-start = ((), (), s32[]{:S(2)}) async-start(), calls=%async_computation | async-start | bytes 8912896 | tf_op jit(solution)/shard_map/all_gather | solution.py:100
  6.5 11.4 %collective-permute-start = (bf16[2,256,512]{2,1,0:T(8,128)(2,1)}, bf16[2,256,512]{2,1,0:T(8,128)(2,1)S(1)}, u32[]{:S(2)}, u32[]{:S(2)}) collective-permute-start(bf16[2,256,512]{2,1,0:T(8,128)(2,1)} %param.6), channel_id=1, source_target_pairs={{0,8},{8,16},{16,24},{24,32},{32,40},{40,48},{48,56},{56,64},{64,7... | collective-permute-start | bytes 1572872 | tf_op jit(solution)/shard_map/ppermute | solution.py:17
  8.0 10.1 %collective-permute-start.1 = (bf16[2,256,512]{2,1,0:T(8,128)(2,1)}, bf16[2,256,512]{2,1,0:T(8,128)(2,1)S(1)}, u32[]{:S(2)}, u32[]{:S(2)}) collective-permute-start(bf16[2,256,512]{2,1,0:T(8,128)(2,1)} %param.6), channel_id=1, source_target_pairs={{8,0},{16,8},{24,16},{32,24},{40,32},{48,40},{56,48},{64,56},{72,6... | collective-permute-start | bytes 1572872 | tf_op jit(solution)/shard_map/ppermute | solution.py:17
  19.0 1.2 copy-start.5
  23.1 149.3 %all-gather.9.cloned.1.call-start = ((), (), s32[]{:S(2)}) async-start(), calls=%async_computation.1 | async-start | bytes 4718592 | tf_op jit(solution)/shard_map/all_gather | solution.py:11
  92.5 7.5 %copy-start.6 = (f32[256,512]{1,0:T(8,128)S(1)}, f32[256,512]{1,0:T(8,128)}, u32[]{:S(2)}) copy-start(f32[256,512]{1,0:T(8,128)} %param.10) | copy-start | bytes 1572868
  99.8 170.0 %all-gather.11.cloned.1.call-start = ((), (), s32[]{:S(2)}) async-start(), calls=%async_computation.2 | async-start | bytes 4718592 | tf_op jit(solution)/shard_map/all_gather | solution.py:11
  200.3 149.9 %all-gather.13.cloned.1.call-start = ((), (), s32[]{:S(2)}) async-start(), calls=%async_computation.3 | async-start | bytes 8912896 | tf_op jit(solution)/shard_map/all_gather | solution.py:100
  291.4 177.3 %all-gather.15.cloned.1.call-start = ((), (), s32[]{:S(2)}) async-start(), calls=%async_computation.4 | async-start | bytes 8912896 | tf_op jit(solution)/shard_map/all_gather | solution.py:100
  362.7 7.8 %copy-start = (bf16[1,4096,512]{2,1,0:T(8,128)(2,1)S(1)}, bf16[1,4096,512]{2,1,0:T(8,128)(2,1)}, u32[]{:S(2)}) copy-start(bf16[1,4096,512]{2,1,0:T(8,128)(2,1)} %copy.76) | copy-start | bytes 12582916
  382.5 4.6 copy-start.1
  382.5 5.9 copy-start.2
  396.4 7.5 %collective-permute-start.3 = (bf16[2,256,512]{2,1,0:T(8,128)(2,1)S(1)}, bf16[2,256,512]{2,1,0:T(8,128)(2,1)}, u32[]{:S(2)}, u32[]{:S(2)}) collective-permute-start(bf16[2,256,512]{2,1,0:T(8,128)(2,1)S(1)} %pad_maximum_fusion.4), channel_id=1, source_target_pairs={{8,0},{16,8},{24,16},{32,24},{40,32},{48,40},{56,48},{64,56},{72,6... | collective-permute-start | bytes 1572872 | tf_op jit(solution)/shard_map/ppermute | solution.py:17
  397.7 6.2 %collective-permute-start.2 = (bf16[2,256,512]{2,1,0:T(8,128)(2,1)S(1)}, bf16[2,256,512]{2,1,0:T(8,128)(2,1)}, u32[]{:S(2)}, u32[]{:S(2)}) collective-permute-start(bf16[2,256,512]{2,1,0:T(8,128)(2,1)S(1)} %pad_maximum_fusion.4), channel_id=1, source_target_pairs={{0,8},{8,16},{16,24},{24,32},{32,40},{40,48},{48,56},{56,64},{64,7... | collective-permute-start | bytes 1572872 | tf_op jit(solution)/shard_map/ppermute | solution.py:17
  410.7 148.4 %all-gather.17.cloned.1.call-start = ((), (), s32[]{:S(2)}) async-start(), calls=%async_computation.5 | async-start | bytes 4718592 | tf_op jit(solution)/shard_map/all_gather | solution.py:11
Sparse Core Ops, SparseCore 0:
  23.2 58.7 all-gather.6
  99.9 72.4 all-gather.8
  200.5 69.2 all-gather.10
  291.5 58.6 all-gather.12
  410.8 57.8 all-gather.14
  486.6 72.4 all-gather.16
